TPU v7x, 128 devices: a whole 4x4x4 slice. The times are simulated.
128 devices in a mesh: section: 2 (over core), seq: 16 (over z, y), head: 4 (over x).
Axes of the slice: x: 4, y: 4, z: 4, core: 2. Of those that a mesh axis runs over, the one named last changes fastest.
Arguments:
- query_vectors: bfloat16 [2, 2048, 8192], P('section', 'seq', 'head'), may hold values from -400 to 400
- key_vectors: bfloat16 [2, 2048, 8192], P('section', 'seq', 'head'), may hold values from -6 to 6
- value_vectors: bfloat16 [2, 2048, 8192], P('section', 'seq', 'head'), may hold values from -6 to 6
- prior_state: float32 [2, 64, 128, 128], P('section', 'head'), may hold values from -128 to 128
- doc_ids: int32 [2, 2048], P('section', 'seq'), may hold values from 0 to 3, never falling along the last dimension, each value on 1 to 1024 neighbouring positions
- norm_gain: float32 [2, 8192], P('section', 'head'), may hold values from 0.25 to 1.75
- residual: bfloat16 [2, 2048, 6144], P('section', 'head', 'seq'), may hold values from -6 to 6
- out_weight: bfloat16 [2, 8192, 6144], P('section', 'head', 'seq'), may hold values from -0.0625 to 0.0625
- enc_weight: bfloat16 [2, 6144, 32768], P('section', None, ('seq', 'head')), may hold values from -0.078125 to 0.078125
- enc_bias: float32 [2, 32768], P('section', ('seq', 'head')), may hold values from -5 to 5
Outputs:
- handoff: bfloat16 [2, 2048, 6144], P('section', 'head', 'seq')
- monitor: bfloat16 [2, 32, 32768], P('section', None, ('seq', 'head'))
Inputs may be any that keep to these rules, and one draw needn't show every extreme that they name: `doc_ids`: document numbers never fall along a section's tokens, are 0 at its first token and rise by at most 1 from one token to the next; a document has at most 1024 tokens, and one has exactly that many.
All inputs are finite; a program needn't handle non-finite values.
Results may differ from a plain program's by a relative error of at most 0.0039.
Values may be sent and summed in bfloat16 or wider, within the bound.
No kernel may reach another device: no remote copies, remote signals or barrier semaphores. Data moves between devices by JAX's collectives and lax.ppermute only.
A program may use at most 128 MiB of HBM per device.

v0:
```python
import jax
import jax.numpy as jnp
from jax import lax
from jax.sharding import PartitionSpec as P

HD = 128
POOL = 64
HDIM = 8192
epsilon = 1e-06


def entering(part, axis, combine, identity):
    place = lax.axis_index(axis)
    gathered = jax.tree.map(lambda a: lax.all_gather(a, axis), part)
    state = jax.tree.map(lambda a, e: jnp.zeros_like(a) + jnp.asarray(e, a.dtype), part, identity)

    def one(hop, state):
        return combine(
            state, jax.tree.map(lambda a: lax.dynamic_index_in_dim(a, hop, 0, False), gathered)
        )

    return lax.fori_loop(0, place, one, state)


def passed_along(x, axis, by):
    devices = lax.axis_size(axis)
    return lax.ppermute(x, axis, [(i, (i + by) % devices) for i in range(devices)])


def merge_states(first_pair, second_pair):
    first_state, first_doc = first_pair
    second_state, second_doc = second_pair
    top_doc = jnp.maximum(first_doc, second_doc)
    merged = jnp.where(first_doc == top_doc, first_state, 0.0) + jnp.where(
        second_doc == top_doc, second_state, 0.0
    )
    return (merged, top_doc)


def local(
    query_vectors,
    key_vectors,
    value_vectors,
    prior_state,
    doc_ids,
    norm_gain,
    residual,
    out_weight,
    enc_weight,
    enc_bias,
):
    highest = lax.Precision.HIGHEST
    row_count = query_vectors.shape[1]
    local_heads = query_vectors.shape[2] // HD
    queries = query_vectors[0].reshape(row_count, local_heads, HD)
    keys_block = key_vectors[0].reshape(row_count, local_heads, HD)
    values_block = value_vectors[0].reshape(row_count, local_heads, HD)
    doc_index = doc_ids[0]
    doc_float = doc_index.astype(jnp.float32)
    last_doc = doc_float[-1]
    keys_last = jnp.where(
        (doc_index == doc_index[-1])[:, None, None], keys_block, jnp.zeros_like(keys_block)
    )
    summary = jnp.einsum(
        "thd,the->hde", keys_last, values_block, preferred_element_type=jnp.float32
    )
    identity_pair = (jnp.zeros_like(summary), jnp.full((1,), -1.0, jnp.float32))
    earlier_state, earlier_last = entering(
        (summary, last_doc[None]), "seq", merge_states, identity_pair
    )
    earlier_doc = earlier_last[0]
    incoming_state, incoming_doc = merge_states(
        (prior_state[0], jnp.zeros((), jnp.float32)), (earlier_state, earlier_doc)
    )
    inter = jnp.einsum(
        "thd,hde->the", queries.astype(jnp.float32), incoming_state, precision=highest
    )
    inter = inter * (doc_float == incoming_doc).astype(jnp.float32)[:, None, None]
    scores = jnp.einsum("thd,uhd->htu", queries, keys_block, preferred_element_type=jnp.float32)
    positions = jnp.arange(row_count)
    same_doc = (positions[None, :] <= positions[:, None]) & (
        doc_index[:, None] == doc_index[None, :]
    )
    scores = jnp.where(same_doc[None, :, :], scores, 0.0)
    intra = jnp.einsum("htu,uhe->the", scores, values_block.astype(jnp.float32), precision=highest)
    attended = (inter + intra).reshape(row_count, local_heads * HD)
    total_square = lax.psum(jnp.sum(attended * attended, axis=1), "head")
    inverse_rms = lax.rsqrt(total_square / HDIM + epsilon)
    normed = (attended * inverse_rms[:, None] * norm_gain[0]).astype(jnp.bfloat16)
    projection = out_weight[0]
    partial_sums = jnp.dot(
        lax.all_gather(normed, "seq", axis=0, tiled=True),
        projection,
        preferred_element_type=jnp.float32,
    )
    own_rows = residual[0]
    encoder = enc_weight[0]
    latent_width = encoder.shape[1]
    reduced = lax.psum_scatter(partial_sums, "head", scatter_dimension=0, tiled=True)
    layer_out = (own_rows.astype(jnp.float32) + reduced).astype(jnp.bfloat16)
    features = lax.all_gather(layer_out, "head", axis=0, tiled=True)
    pre_scores = jnp.dot(
        lax.all_gather(features, "seq", axis=1, tiled=True),
        encoder,
        preferred_element_type=jnp.float32,
    )
    latent = jax.nn.relu(pre_scores + enc_bias[0])
    pooled = jnp.mean(latent.reshape(-1, POOL, latent_width), axis=1).astype(jnp.bfloat16)
    handoff, monitor = passed_along((layer_out[None], pooled[None]), "section", 1)
    return (handoff, monitor)


def solution(mesh):
    return jax.shard_map(
        local,
        mesh=mesh,
        in_specs=(
            P("section", "seq", "head"),
            P("section", "seq", "head"),
            P("section", "seq", "head"),
            P("section", "head", None, None),
            P("section", "seq"),
            P("section", "head"),
            P("section", "head", "seq"),
            P("section", "head", "seq"),
            P("section", None, ("seq", "head")),
            P("section", ("seq", "head")),
        ),
        out_specs=(P("section", "head", "seq"), P("section", None, ("seq", "head"))),
        check_vma=False,
    )
```

profile of v0, /device:TPU:1, one launch (start us, length us, event | category | flops | bytes accessed | tf_op | source)
XLA Modules:
  0.0 542.9 jit_solution(13562496052584884869)
XLA Ops:
  7.2 1.3 slice.8
  8.6 1.3 broadcast_compare_fusion
  9.9 1.3 copy.23
  11.2 1.3 copy.24
  12.5 1.5 fusion.14
  14.1 1.2 dynamic-slice
  16.0 0.8 slice_dynamic-update-slice_fusion
  16.8 35.9 %all-reduce = f32[16]{0:T(128)S(1)} all-reduce(f32[16]{0:T(128)S(1)} %slice_dynamic-update-slice_fusion), channel_id=2, replica_groups=mesh['section'=2,'seq'=16,'head'=4] {'seq'}, use_global_device_ids=true, to_apply=%add | all-reduce | flops 16 | bytes 128
  52.8 1.1 copy.25
  54.3 2.2 convolution_bitcast_fusion
  56.5 72.5 %all-gather.13.cloned.1.call-done = f32[256,128,128]{2,1,0:T(8,128)} async-done(((f32[16,128,128]{2,1,0:T(8,128)}), f32[256,128,128]{2,1,0:T(8,128)}) %all-gather.13.cloned.1.call-update) | async-done | bytes 16777232 | tf_op jit(solution)/shard_map/all_gather | solution.py:14
  129.1 3.6 multiply_reduce_fusion
  132.7 8.4 %psum.7 = f32[128]{0:T(128)S(1)} all-reduce(f32[128]{0:T(128)S(1)} %get-tuple-element.50), channel_id=1, replica_groups=mesh['section'=2,'seq'=16,'head'=4] {'head'}, use_global_device_ids=true, to_apply=%region_3.4 | all-reduce | flops 128 | bytes 1024 | tf_op jit(solution)/shard_map/psum | solution.py:87
  141.1 2.4 fusion.9
  143.6 128.4 %all-gather.7.cloned.1.call-done = bf16[2048,2048]{0,1:T(8,128)(2,1)} async-done(((bf16[128,2048]{0,1:T(8,128)(2,1)}), bf16[2048,2048]{0,1:T(8,128)(2,1)}) %all-gather.7.cloned.1.call-update) | async-done | bytes 8388624 | tf_op jit(solution)/shard_map/all_gather | solution.py:92
  272.0 8.7 %fusion.4 = f32[2048,384]{1,0:T(8,128)} fusion(bf16[2048,2048]{0,1:T(8,128)(2,1)} %all-gather.7.cloned.1.call-done, bf16[1,2048,384]{2,1,0:T(8,128)(2,1)S(1)} %copy-done), kind=kOutput, calls=%fused_computation.6 | convolution fusion | flops 3221225472 | bytes 13107200 | tf_op jit(solution)/shard_map/dot_general | solution.py:91
  280.7 38.5 %reduce-scatter.2.cloned.1.call-done = f32[512,384]{1,0:T(8,128)} async-done(((f32[2048,384]{1,0:T(8,128)}), f32[512,384]{1,0:T(8,128)}) %reduce-scatter.2.cloned.1.call-update) | async-done | bytes 786448 | tf_op jit(solution)/shard_map/reduce_scatter | solution.py:99
  319.2 1.9 fusion.12
  321.2 26.3 %all-gather.9.cloned.1.call-done = bf16[2048,384]{1,0:T(8,128)(2,1)} async-done(((bf16[512,384]{1,0:T(8,128)(2,1)}), bf16[2048,384]{1,0:T(8,128)(2,1)}) %all-gather.9.cloned.1.call-update) | async-done | bytes 1572880 | tf_op jit(solution)/shard_map/all_gather | solution.py:101
  347.6 0.8 collective-permute-start
  348.3 164.4 %all-gather.11.cloned.1.call-done = bf16[2048,6144]{1,0:T(8,128)(2,1)} async-done(((bf16[2048,384]{1,0:T(8,128)(2,1)}), bf16[2048,6144]{1,0:T(8,128)(2,1)}) %all-gather.11.cloned.1.call-update) | async-done | bytes 25165840 | tf_op jit(solution)/shard_map/all_gather | solution.py:103
  512.7 19.8 %bitcast_reduce_fusion = f32[32,512]{1,0:T(8,128)S(1)} fusion(bf16[2048,6144]{1,0:T(8,128)(2,1)} %all-gather.11.cloned.1.call-done, bf16[1,6144,512]{2,1,0:T(8,128)(2,1)} %param.20, f32[512]{0:T(512)S(1)} %bitcast.80), kind=kOutput, calls=%fused_computation.4 | convolution fusion | flops 12888031232 | bytes 31524864 | tf_op jit(solution)/shard_map/dot_general | solution.py:102
  532.5 1.6 collective-permute-start.1
  534.1 0.9 collective-permute-done.1
  (34 shorter events, 2.8 us)
Async XLA Ops:
  7.2 264.8 %copy-start = (bf16[1,2048,384]{2,1,0:T(8,128)(2,1)S(1)}, bf16[1,2048,384]{2,1,0:T(8,128)(2,1)}, u32[]{:S(2)}) copy-start(bf16[1,2048,384]{2,1,0:T(8,128)(2,1)} %param.19) | copy-start | bytes 4718596
  7.2 46.7 %copy-start.4 = (s32[1,128]{1,0:T(1,128)S(1)}, s32[1,128]{1,0:T(1,128)}, u32[]{:S(2)}) copy-start(s32[1,128]{1,0:T(1,128)} %param.16) | copy-start | bytes 1540
  7.2 121.8 %all-gather.13.cloned.1.call-start = ((), (), s32[]{:S(2)}) async-start(), calls=%async_computation.5 | async-start | bytes 17825792 | tf_op jit(solution)/shard_map/all_gather | solution.py:14
  14.1 257.9 %all-gather.7.cloned.1.call-start = ((), (), s32[]{:S(2)}) async-start(), calls=%async_computation.1 | async-start | bytes 8912896 | tf_op jit(solution)/shard_map/all_gather | solution.py:92
  129.1 12.0 %copy-start.3 = (f32[1,2048]{1,0:T(1,128)S(1)}, f32[1,2048]{1,0:T(1,128)}, u32[]{:S(2)}) copy-start(f32[1,2048]{1,0:T(1,128)} %param.17) | copy-start | bytes 24580
  143.5 175.7 %copy-start.2 = (bf16[1,512,384]{2,1,0:T(8,128)(2,1)S(1)}, bf16[1,512,384]{2,1,0:T(8,128)(2,1)}, u32[]{:S(2)}) copy-start(bf16[1,512,384]{2,1,0:T(8,128)(2,1)} %param.18) | copy-start | bytes 1179652
  143.5 175.6 %reduce-scatter.2.cloned.1.call-start = ((), (), s32[]{:S(2)}) async-start(), calls=%async_computation.2 | async-start | bytes 3932160 | tf_op jit(solution)/shard_map/reduce_scatter | solution.py:99
  280.7 232.0 %copy-start.5 = (f32[1,512]{1,0:T(1,128)S(1)}, f32[1,512]{1,0:T(1,128)}, u32[]{:S(2)}) copy-start(f32[1,512]{1,0:T(1,128)} %param.21) | copy-start | bytes 6148
  280.7 66.8 %all-gather.9.cloned.1.call-start = ((), (), s32[]{:S(2)}) async-start(), calls=%async_computation.3 | async-start | bytes 1966080 | tf_op jit(solution)/shard_map/all_gather | solution.py:101
  321.2 191.5 %all-gather.11.cloned.1.call-start = ((), (), s32[]{:S(2)}) async-start(), calls=%async_computation.4 | async-start | bytes 26738688 | tf_op jit(solution)/shard_map/all_gather | solution.py:103
  347.6 186.6 %collective-permute-start = (bf16[1,512,384]{2,1,0:T(8,128)(2,1)}, bf16[1,512,384]{2,1,0:T(8,128)(2,1)S(1)}, u32[]{:S(2)}, u32[]{:S(2)}) collective-permute-start(bf16[1,512,384]{2,1,0:T(8,128)(2,1)} %bitcast.76), channel_id=1, source_target_pairs={{0,64},{64,0},{1,65},{65,1},{2,66},{66,2},{3,67},{67,3},{4,68},{68... | collective-permute-start | bytes 1179656 | tf_op jit(solution)/shard_map/ppermute | solution.py:27
  512.7 23.7 %copy-start.1 = (bf16[1,2048,384]{2,1,0:T(8,128)(2,1)S(1)}, bf16[1,2048,384]{2,1,0:T(8,128)(2,1)}, u32[]{:S(2)}) copy-start(bf16[1,2048,384]{2,1,0:T(8,128)(2,1)} %param.19) | copy-start | bytes 4718596
  532.5 2.5 collective-permute-start.1
Sparse Core Ops, SparseCore 0:
  14.2 114.7 all-gather.12
  143.7 128.2 all-gather.6
  280.8 38.3 reduce-scatter.1
  321.3 26.1 all-gather.8
  349.5 163.1 all-gather.10
where the time goes:
time: 544 us; the launch traced here: 543 us
  waiting for transfers between devices  431 us (79%)
  blocking collectives  44.3 us (8%)
  matrix products  36.1 us (7%)
  between operations  13.9 us (3%)
  local copies, waits for them, and re-layouts  8.65 us (2%)
  other arithmetic  6.43 us (1%)
    all_gather x1, waiting for transfers between devices, local(): lax.all_gather(features, 'seq', axis=1, tiled=True)  164 us
    all_gather x1, waiting for transfers between devices, local(): lax.all_gather(normed, 'seq', axis=0, tiled=True)  128 us
    all_gather x1, waiting for transfers between devices, entering(): gathered = jax.tree.map(lambda a: lax.all_gather(a, axis), part)  72.5 us
    reduce_scatter x1, waiting for transfers between devices, local(): lax.psum_scatter(partial_sums, 'head', scatter_dimension=0, tiled=True)  38.5 us
    unnamed x1, blocking collectives  35.9 us
    all_gather x1, waiting for transfers between devices, local(): features = lax.all_gather(layer_out, 'head', axis=0, tiled=True)  26.3 us
    dot_general x1, matrix products, local(): jnp.dot(lax.all_gather(features, 'seq', axis=1, tiled=True), encoder, pre...  19.8 us
  transfers between devices with their start and end apart: 7, of which 6 were waited for; matrix products, arithmetic and copies ran while one was open for 5% of the time, Pallas kernels for 0%

commit v1 on v0

--- a/solution.py
+++ b/solution.py
@@ -100,7 +100,9 @@
     layer_out = (own_rows.astype(jnp.float32) + reduced).astype(jnp.bfloat16)
     features = lax.all_gather(layer_out, "head", axis=0, tiled=True)
     pre_scores = jnp.dot(
-        lax.all_gather(features, "seq", axis=1, tiled=True),
+        jnp.concatenate(
+            lax.all_to_all(jnp.stack([features] * lax.axis_size("seq")), "seq", 0, 0), axis=1
+        ),
         encoder,
         preferred_element_type=jnp.float32,
     )

time: 544 us -> 772 us (1.42)
  waiting for transfers between devices: 431 us -> 640 us
  local copies, waits for them, and re-layouts: 8.65 us -> 19 us
    all_to_all x0 -> x1, waiting for transfers between devices: none -> 374 us  [local(): lax.all_to_all(jnp.stack([features] * lax.axis_size('seq')), 'seq', 0, 0)]
    all_gather x1 -> x0, waiting for transfers between devices: 164 us -> none  [local(): lax.all_gather(features, 'seq', axis=1, tiled=True)]
    another operation x0 -> x1, local copies, waits for them, and re-layouts: none -> 8.65 us  [local(): jnp.stack([features] * lax.axis_size('seq'))]
  transfers between devices with their start and end apart: 7 -> 7, of which waited for: 6 -> 6; matrix products, arithmetic and copies ran while one was open for 5% -> 3% of each run, Pallas kernels for 0% -> 0%
where the time goes in v1:
time: 772 us; the launch traced here: 770 us
  waiting for transfers between devices  640 us (83%)
  blocking collectives  44.3 us (6%)
  matrix products  36.1 us (5%)
  local copies, waits for them, and re-layouts  19 us (2%)
  between operations  13.9 us (2%)
  starting transfers between devices  10.2 us (1%)
    all_to_all x1, waiting for transfers between devices, local(): lax.all_to_all(jnp.stack([features] * lax.axis_size('seq')), 'seq', 0, 0)  374 us
    all_gather x1, waiting for transfers between devices, local(): lax.all_gather(normed, 'seq', axis=0, tiled=True)  128 us
    all_gather x1, waiting for transfers between devices, entering(): gathered = jax.tree.map(lambda a: lax.all_gather(a, axis), part)  72.5 us
    reduce_scatter x1, waiting for transfers between devices, local(): lax.psum_scatter(partial_sums, 'head', scatter_dimension=0, tiled=True)  38.5 us
    unnamed x1, blocking collectives  35.9 us
    all_gather x1, waiting for transfers between devices, local(): features = lax.all_gather(layer_out, 'head', axis=0, tiled=True)  26.4 us
    dot_general x1, matrix products, local(): jnp.dot(jnp.concatenate(lax.all_to_all(jnp.stack([features] * lax.axis_si...  19.9 us
  transfers between devices with their start and end apart: 7, of which 6 were waited for; matrix products, arithmetic and copies ran while one was open for 3% of the time, Pallas kernels for 0%

profile of v1, /device:TPU:1, one launch (start us, length us, event | category | flops | bytes accessed | tf_op | source)
XLA Modules:
  0.0 770.2 jit_solution(3780598518025714011)
XLA Ops:
  7.2 1.3 slice.8
  8.6 1.3 broadcast_compare_fusion
  9.9 1.3 copy.32
  11.2 1.3 copy.33
  12.5 1.5 fusion.14
  14.1 1.2 dynamic-slice
  16.8 35.9 %all-reduce = f32[16]{0:T(128)S(1)} all-reduce(f32[16]{0:T(128)S(1)} %slice_dynamic-update-slice_fusion), channel_id=2, replica_groups=mesh['section'=2,'seq'=16,'head'=4] {'seq'}, use_global_device_ids=true, to_apply=%add | all-reduce | flops 16 | bytes 128
  54.3 2.2 convolution_bitcast_fusion
  56.5 72.5 %all-gather.10.cloned.1.call-done = f32[256,128,128]{2,1,0:T(8,128)} async-done(((f32[16,128,128]{2,1,0:T(8,128)}), f32[256,128,128]{2,1,0:T(8,128)}) %all-gather.10.cloned.1.call-update) | async-done | bytes 16777232 | tf_op jit(solution)/shard_map/all_gather | solution.py:14
  129.1 3.6 multiply_reduce_fusion
  132.7 8.4 %psum.7 = f32[128]{0:T(128)S(1)} all-reduce(f32[128]{0:T(128)S(1)} %get-tuple-element.50), channel_id=1, replica_groups=mesh['section'=2,'seq'=16,'head'=4] {'head'}, use_global_device_ids=true, to_apply=%region_3.4 | all-reduce | flops 128 | bytes 1024 | tf_op jit(solution)/shard_map/psum | solution.py:87
  141.1 2.4 fusion.9
  143.6 128.4 %all-gather.6.cloned.1.call-done = bf16[2048,2048]{0,1:T(8,128)(2,1)} async-done(((bf16[128,2048]{0,1:T(8,128)(2,1)}), bf16[2048,2048]{0,1:T(8,128)(2,1)}) %all-gather.6.cloned.1.call-update) | async-done | bytes 8388624 | tf_op jit(solution)/shard_map/all_gather | solution.py:92
  272.0 8.7 %fusion.4 = f32[2048,384]{1,0:T(8,128)} fusion(bf16[2048,2048]{0,1:T(8,128)(2,1)} %all-gather.6.cloned.1.call-done, bf16[1,2048,384]{2,1,0:T(8,128)(2,1)S(1)} %copy-done), kind=kOutput, calls=%fused_computation.6 | convolution fusion | flops 3221225472 | bytes 13107200 | tf_op jit(solution)/shard_map/dot_general | solution.py:91
  280.7 38.5 %reduce-scatter.2.cloned.1.call-done = f32[512,384]{1,0:T(8,128)} async-done(((f32[2048,384]{1,0:T(8,128)}), f32[512,384]{1,0:T(8,128)}) %reduce-scatter.2.cloned.1.call-update) | async-done | bytes 786448 | tf_op jit(solution)/shard_map/reduce_scatter | solution.py:99
  319.2 1.9 fusion.12
  321.2 26.4 %all-gather.8.cloned.1.call-done = bf16[2048,384]{1,0:T(8,128)(2,1)} async-done(((bf16[512,384]{1,0:T(8,128)(2,1)}), bf16[2048,384]{1,0:T(8,128)(2,1)}) %all-gather.8.cloned.1.call-update) | async-done | bytes 1572880 | tf_op jit(solution)/shard_map/all_gather | solution.py:101
  347.5 1.7 copy.30
  349.2 8.7 %stack.2 = bf16[16,2048,384]{1,2,0:T(8,128)(2,1)} broadcast(bf16[2048,384]{0,1:T(8,128)(2,1)S(1)} %copy.30), dimensions={1,2} | broadcast | bytes 26738688 | tf_op jit(solution)/shard_map/stack | solution.py:104
  357.9 6.9 all-to-all-start
  364.8 1.2 collective-permute-start
  366.0 373.7 %all-to-all-done = bf16[16,2048,384]{1,2,0:T(8,128)(2,1)} async-done(((bf16[16,2048,384]{1,2,0:T(8,128)(2,1)}), bf16[16,2048,384]{1,2,0:T(8,128)(2,1)}, u32[]{:S(2)}, u32[]{:S(2)}) %all-to-all-start) | async-done | bytes 25165856 | tf_op jit(solution)/shard_map/all_to_all | solution.py:104
  739.7 19.9 %bitcast_reduce_fusion = f32[32,512]{1,0:T(8,128)S(1)} fusion(bf16[2048,6144]{0,1:T(8,128)(2,1)} %bitcast.19, bf16[1,6144,512]{2,1,0:T(8,128)(2,1)} %param.20, f32[512]{0:T(512)S(1)} %bitcast.83), kind=kOutput, calls=%fused_computation.4 | convolution fusion | flops 12888031232 | bytes 31524864 | tf_op jit(solution)/shard_map/dot_general | solution.py:102
  759.6 1.9 collective-permute-start.1
  (37 shorter events, 5.6 us)
Async XLA Ops:
  7.2 264.8 %copy-start = (bf16[1,2048,384]{2,1,0:T(8,128)(2,1)S(1)}, bf16[1,2048,384]{2,1,0:T(8,128)(2,1)}, u32[]{:S(2)}) copy-start(bf16[1,2048,384]{2,1,0:T(8,128)(2,1)} %param.19) | copy-start | bytes 4718596
  7.2 46.7 %copy-start.5 = (s32[1,128]{1,0:T(1,128)S(1)}, s32[1,128]{1,0:T(1,128)}, u32[]{:S(2)}) copy-start(s32[1,128]{1,0:T(1,128)} %param.16) | copy-start | bytes 1540
  7.2 121.8 %all-gather.10.cloned.1.call-start = ((), (), s32[]{:S(2)}) async-start(), calls=%async_computation.5 | async-start | bytes 17825792 | tf_op jit(solution)/shard_map/all_gather | solution.py:14
  14.0 257.9 %all-gather.6.cloned.1.call-start = ((), (), s32[]{:S(2)}) async-start(), calls=%async_computation.2 | async-start | bytes 8912896 | tf_op jit(solution)/shard_map/all_gather | solution.py:92
  129.1 12.0 %copy-start.4 = (f32[1,2048]{1,0:T(1,128)S(1)}, f32[1,2048]{1,0:T(1,128)}, u32[]{:S(2)}) copy-start(f32[1,2048]{1,0:T(1,128)} %param.17) | copy-start | bytes 24580
  143.5 175.7 %copy-start.3 = (bf16[1,512,384]{2,1,0:T(8,128)(2,1)S(1)}, bf16[1,512,384]{2,1,0:T(8,128)(2,1)}, u32[]{:S(2)}) copy-start(bf16[1,512,384]{2,1,0:T(8,128)(2,1)} %param.18) | copy-start | bytes 1179652
  143.5 175.6 %reduce-scatter.2.cloned.1.call-start = ((), (), s32[]{:S(2)}) async-start(), calls=%async_computation.3 | async-start | bytes 3932160 | tf_op jit(solution)/shard_map/reduce_scatter | solution.py:99
  280.7 66.8 %all-gather.8.cloned.1.call-start = ((), (), s32[]{:S(2)}) async-start(), calls=%async_computation.4 | async-start | bytes 1966080 | tf_op jit(solution)/shard_map/all_gather | solution.py:101
  357.9 6.9 copy-start.2
  357.9 381.8 %copy-start.6 = (f32[1,512]{1,0:T(1,128)S(1)}, f32[1,512]{1,0:T(1,128)}, u32[]{:S(2)}) copy-start(f32[1,512]{1,0:T(1,128)} %param.21) | copy-start | bytes 6148
  357.9 381.8 %all-to-all-start = ((bf16[16,2048,384]{1,2,0:T(8,128)(2,1)}), bf16[16,2048,384]{1,2,0:T(8,128)(2,1)}, u32[]{:S(2)}, u32[]{:S(2)}) async-start(bf16[16,2048,384]{1,2,0:T(8,128)(2,1)} %stack.2), calls=%async_computation.1 | async-start | bytes 50331648 | tf_op jit(solution)/shard_map/all_to_all | solution.py:104
  364.8 396.7 %collective-permute-start = (bf16[1,512,384]{2,1,0:T(8,128)(2,1)S(1)}, bf16[1,512,384]{2,1,0:T(8,128)(2,1)S(1)}, u32[]{:S(2)}, u32[]{:S(2)}) collective-permute-start(bf16[1,512,384]{2,1,0:T(8,128)(2,1)S(1)} %bitcast.79), channel_id=1, source_target_pairs={{0,64},{64,0},{1,65},{65,1},{2,66},{66,2},{3,67},{67,3},{4,68},{68... | collective-permute-start | bytes 1179656 | tf_op jit(solution)/shard_map/ppermute | solution.py:27
  739.7 24.0 %copy-start.1 = (bf16[1,2048,384]{2,1,0:T(8,128)(2,1)S(1)}, bf16[1,2048,384]{2,1,0:T(8,128)(2,1)}, u32[]{:S(2)}) copy-start(bf16[1,2048,384]{2,1,0:T(8,128)(2,1)} %param.19) | copy-start | bytes 4718596
  759.6 2.8 collective-permute-start.1
Sparse Core Ops, SparseCore 0:
  14.2 114.7 all-gather.9
  143.6 128.2 all-gather.5
  280.8 38.3 reduce-scatter.1
  321.3 26.1 all-gather.7
